TPU v7x, 128 devices: a whole 4x4x4 slice. The times are simulated.
128 devices in a mesh: seq: 8 (over y_lo, z), chan: 16 (over x, y_hi, core).
Axes of the slice: x: 4, y: 4 (y_hi: 2, y_lo: 2; y = y_hi * 2 + y_lo), z: 4, core: 2. Of those that a mesh axis runs over, the one named last changes fastest.
Arguments:
- resid: bfloat16 [16384, 4096], P('seq', 'chan'), may hold values from -1100 to 1100
- norm_gain: bfloat16 [4096], P('chan'), may hold values from 0.5 to 1.5
- feat_weight: bfloat16 [4096, 3, 4096], P(None, None, 'chan'), may hold values from -0.09375 to 0.09375
- short_filter: float32 [3, 3, 4096], P(None, None, 'chan'), may hold values from -3.5 to 3.5
- mr_filter: bfloat16 [128, 4096], P(None, 'chan'), may hold values from -0.5 to 0.5
- gates_lr: bfloat16 [16384, 2, 4096], P('seq', None, 'chan'), may hold values from -6 to 6
- decay_rate: float32 [16, 4096], P(None, 'chan'), may hold values from 1.2207031e-06 to 0.0333333333
- residue: float32 [16, 4096], P(None, 'chan'), may hold values from -1.5 to 1.5
- skip_gain: float32 [4096], P('chan'), may hold values from 0.5 to 1.5
Outputs:
- mixed: bfloat16 [16384, 4096], P('seq', 'chan')
All inputs are finite; a program needn't handle non-finite values.
Results may differ from a plain program's by a relative error of at most 0.012.
Values may be sent and summed in bfloat16 or wider, within the bound.
A program may use at most 128 MiB of HBM per device.

v0:
```python
import jax
import jax.numpy as jnp
from jax import lax
from jax.sharding import PartitionSpec as P

D = 4096
tile_rows = 128
norm_epsilon = 1e-05
highest = lax.Precision.HIGHEST


def shifted(value, axis, by):
    peers = lax.axis_size(axis)
    pairs = [(i, i + by) for i in range(peers) if 0 <= i + by < peers]
    return lax.ppermute(value, axis, pairs)


def as_sent(value):

    def short(part):
        return part.astype(jnp.bfloat16) if part.dtype == jnp.float32 else part

    return jax.tree.map(short, value)


def combine_states(earlier, later):
    return (earlier[0] * later[0], later[0] * earlier[1] + later[1])


def featurize(padded, short_filter, count):
    short_len = short_filter.shape[0]
    total = jnp.zeros((count,) + padded.shape[1:], jnp.float32)
    for tap_index in range(short_len):
        start_row = short_len - 1 - tap_index
        total = (
            total
            + padded[start_row : start_row + count].astype(jnp.float32)
            * short_filter[tap_index][None]
        )
    return total


def depthwise(signal, taps, front, precision_kind, out_type):
    channels = signal.shape[2]
    kernel = taps[::-1][:, None, :]
    return lax.conv_general_dilated(
        signal,
        kernel,
        (1,),
        ((front, 0),),
        dimension_numbers=("NWC", "WIO", "NWC"),
        feature_group_count=channels,
        precision=precision_kind,
        preferred_element_type=out_type,
    )


def medium_conv(z_full, mr_filter, length):
    result = depthwise(z_full[None], mr_filter, 0, None, jnp.float32)
    return result[0, :length]


def modal_local(z_long, decays, residues):
    length, channels = z_long.shape
    blocks = length // tile_rows
    values = z_long.astype(jnp.float32).reshape(blocks, tile_rows, channels)
    offsets = jnp.arange(tile_rows, dtype=jnp.float32)
    weighted = residues * jnp.sqrt(-jnp.expm1(-2.0 * decays))
    powers = jnp.exp(-decays[None] * offsets[:, None, None])
    tap_values = jnp.sum(powers * weighted[None], axis=1)
    within = depthwise(values, tap_values, tile_rows - 1, highest, jnp.float32)
    end_powers = jnp.exp(-decays[None] * (tile_rows - 1.0 - offsets)[:, None, None])
    block_ends = jnp.sum(end_powers[None] * values[:, :, None, :], axis=1)
    step_decay = jnp.broadcast_to(jnp.exp(-decays * tile_rows)[None], block_ends.shape)
    _, inclusive = lax.associative_scan(combine_states, (step_decay, block_ends), axis=0)
    starts = jnp.concatenate([jnp.zeros_like(inclusive[:1]), inclusive[:-1]], axis=0)
    return (within, starts, inclusive[-1])


def modal_finish(within, starts, incoming, decays, residues):
    blocks, _, channels = within.shape
    offsets = jnp.arange(tile_rows, dtype=jnp.float32)
    weighted = residues * jnp.sqrt(-jnp.expm1(-2.0 * decays))
    block_index = jnp.arange(blocks, dtype=jnp.float32)
    starts = (
        starts + jnp.exp(-decays[None] * (tile_rows * block_index)[:, None, None]) * incoming[None]
    )
    out_powers = weighted[None] * jnp.exp(-decays[None] * (offsets + 1.0)[:, None, None])
    carried = jnp.sum(out_powers[None] * starts[:, None, :, :], axis=2)
    return (within + carried).reshape(blocks * tile_rows, channels)


def on_device(
    resid, norm_gain, feat_weight, short_filter, mr_filter, gates_lr, decay_rate, residue, skip_gain
):
    tokens, channels = resid.shape
    flat_weight = feat_weight.reshape(feat_weight.shape[0], 3 * channels)
    values = resid.astype(jnp.float32)
    squares = lax.psum(jnp.sum(values * values, axis=1), "chan")
    inv_scale = lax.rsqrt(squares / D + norm_epsilon)
    normed = (values * inv_scale[:, None] * norm_gain.astype(jnp.float32)[None]).astype(
        jnp.bfloat16
    )
    projected = jnp.dot(
        lax.all_gather(normed, "chan", axis=1, tiled=True),
        flat_weight,
        preferred_element_type=jnp.float32,
    )
    stream_rows = projected.astype(jnp.bfloat16).reshape(tokens, 3, channels)
    short_len = short_filter.shape[0]
    tap_count = mr_filter.shape[0]
    head_rows = shifted(stream_rows[tokens - (short_len - 1) :], "seq", 1)
    featured = featurize(jnp.concatenate([head_rows, stream_rows], axis=0), short_filter, tokens)
    product = (featured[:, 1] * featured[:, 2]).astype(jnp.bfloat16)
    rim_rows = shifted(product[tokens - (tap_count - 1) :], "seq", 1)
    query_gate = featured[:, 0]
    z_full = jnp.concatenate([rim_rows, product], axis=0)
    medium = medium_conv(z_full, mr_filter, tokens)
    mixed_mr = (query_gate * medium).astype(jnp.bfloat16)
    gates = gates_lr.astype(jnp.float32)
    long_input = (gates[:, 1] * mixed_mr.astype(jnp.float32)).astype(jnp.bfloat16)
    spread = lax.all_to_all(long_input, "seq", split_axis=1, concat_axis=0, tiled=True)
    narrow = spread.shape[1]
    first_channel = lax.axis_index("seq") * narrow
    decay_part = lax.dynamic_slice_in_dim(decay_rate, first_channel, narrow, 1)
    residue_part = lax.dynamic_slice_in_dim(residue, first_channel, narrow, 1)
    within, starts, _ = modal_local(spread, decay_part, residue_part)
    whole_conv = modal_finish(within, starts, jnp.zeros_like(decay_part), decay_part, residue_part)
    long_out = lax.all_to_all(
        as_sent(whole_conv), "seq", split_axis=0, concat_axis=1, tiled=True
    ).astype(whole_conv.dtype)
    return (gates[:, 0] * (long_out + skip_gain[None] * long_input.astype(jnp.float32))).astype(
        jnp.bfloat16
    )


def solution(mesh):
    in_specs = (
        P("seq", "chan"),
        P("chan"),
        P(None, None, "chan"),
        P(None, None, "chan"),
        P(None, "chan"),
        P("seq", None, "chan"),
        P(None, "chan"),
        P(None, "chan"),
        P("chan"),
    )
    out_specs = P("seq", "chan")
    return jax.shard_map(
        on_device, mesh=mesh, in_specs=in_specs, out_specs=out_specs, check_vma=False
    )
```

profile of v0, /device:TPU:1, one launch (start us, length us, event | category | flops | bytes accessed | tf_op | source)
XLA Modules:
  0.0 613.1 jit_solution(5045128516159069623)
XLA Ops:
  8.1 34.7 %psum.7 = f32[2048]{0:T(1024)S(1)} all-reduce(f32[2048]{0:T(1024)S(1)} %fusion.2), channel_id=1, replica_groups=mesh['seq'=8,'chan'=16] {'chan'}, use_global_device_ids=true, to_apply=%region_1.0 | all-reduce | flops 2048 | bytes 16384 | tf_op jit(solution)/shard_map/psum | solution.py:99
  46.1 8.7 %copy.172 = bf16[4096,3,256]{0,2,1:T(8,128)(2,1)} copy(bf16[4096,3,256]{2,0,1:T(8,128)(2,1)} %param.11) | data formatting | bytes 12582912 | tf_op args[2]
  54.8 117.1 %all-gather.2.cloned.1.call-done = bf16[2048,4096]{1,0:T(8,128)(2,1)} async-done(((bf16[2048,256]{1,0:T(8,128)(2,1)}), bf16[2048,4096]{1,0:T(8,128)(2,1)}) %all-gather.2.cloned.1.call-update) | async-done | bytes 16777232 | tf_op jit(solution)/shard_map/all_gather | solution.py:105
  171.9 18.2 %convolution_convert_fusion = bf16[2048,768]{1,0:T(8,128)(2,1)S(1)} fusion(bf16[2048,4096]{1,0:T(8,128)(2,1)} %all-gather.2.cloned.1.call-done, bf16[4096,768]{0,1:T(8,128)(2,1)} %bitcast.84), kind=kOutput, calls=%fused_computation.3 | convolution fusion | flops 12886474752 | bytes 26214400 | tf_op jit(solution)/shard_map/dot_general | solution.py:104
  195.1 4.7 copy.173
  199.9 8.2 %multiply_add_fusion = f32[2048,3,256]{0,2,1:T(8,128)S(1)} fusion(bf16[2048,3,256]{0,2,1:T(8,128)(2,1)} %bitcast.76, bf16[2,3,256]{0,2,1:T(8,128)(2,1)S(1)} %collective-permute-done, f32[3,256]{1,0:T(4,128)S(1)} %get-tuple-element.19, f32[3,256]{1,0:T(4,128)S(1)} %get-tuple-element.20, f32[3,256]{1,0:T(4,128)S(1)} %get-tuple-element.18), kind=kLoop, calls=%fused_computation.2 | loop fusion | flops 22020096 | bytes 9449472 | tf_op jit(solution)/shard_map/add | solution.py:36
  214.9 4.7 copy.171
  225.6 47.9 %fusion.17 = f32[8,272,256]{2,0,1:T(8,128)S(1)} fusion(pred[8,272]{0,1:T(8,128)(4,1)S(1)} %copy-done.19, bf16[128,1,256]{2,0,1:T(8,128)(2,1)S(1)} %bitcast.90, bf16[8,399,256]{2,0,1:T(8,128)(2,1)S(1)} %fusion.44), kind=kOutput, calls=%fused_computation.34 | convolution fusion | flops 143163392 | bytes 3930240 | tf_op jit(solution)/shard_map/conv_general_dilated | solution.py:46
  278.6 4.3 multiply_convert_fusion
  282.9 4.8 all-to-all-start
  290.7 10.6 %all-to-all-done = bf16[2048,8,32]{0,2,1:T(8,128)(2,1)S(1)} async-done(((bf16[2048,8,32]{0,2,1:T(8,128)(2,1)}), bf16[2048,8,32]{0,2,1:T(8,128)(2,1)S(1)}, u32[]{:S(2)}, u32[]{:S(2)}) %all-to-all-start) | async-done | bytes 1048608 | tf_op jit(solution)/shard_map/all_to_all | solution.py:122
  305.0 9.3 %multiply_reduce_fusion.1 = f32[128,16,32]{2,1,0:T(8,128)S(1)} fusion(f32[128,128,32]{1,2,0:T(8,128)S(1)} %copy.184, f32[128,16,32]{0,2,1:T(8,128)S(1)} %get-tuple-element.21), kind=kLoop, calls=%fused_computation.1 | loop fusion | flops 16711680 | bytes 2621440 | tf_op jit(solution)/shard_map/reduce_sum | solution.py:73
  321.6 3.7 slice.212
  325.3 3.8 slice.213
  362.8 4.5 slice.246
  382.7 6.6 %pad.51 = f32[16,16,32]{0,2,1:T(8,128)S(1)} pad(f32[8,16,32]{0,2,1:T(8,128)} %add.145, f32[]{:T(128)} %constant.12.clone.1), padding=1_0_1x0_0_0x0_0_0 | pad | bytes 49156 | tf_op jit(solution)/shard_map/pad | solution.py:75
  400.4 7.6 %pad.55 = f32[64,16,32]{0,2,1:T(8,128)S(1)} pad(f32[32,16,32]{0,2,1:T(8,128)} %add.149, f32[]{:T(128)} %constant.12.clone.1), padding=1_0_1x0_0_0x0_0_0 | pad | bytes 196612 | tf_op jit(solution)/shard_map/pad | solution.py:75
  408.7 10.6 %pad.126 = f32[128,16,32]{0,2,1:T(8,128)} pad(f32[64,16,32]{0,2,1:T(8,128)} %add.151, f32[]{:T(128)} %constant.12.clone.1), padding=1_0_1x0_0_0x0_0_0 | pad | bytes 393220
  421.8 5.3 pad.82
  427.9 13.2 %multiply_reduce_fusion = f32[128,128,32]{1,2,0:T(8,128)} fusion(f32[128,16,32]{2,1,0:T(8,128)S(1)} %copy.191, f32[128,16,32]{0,2,1:T(8,128)} %get-tuple-element.16), kind=kLoop, calls=%fused_computation | loop fusion | flops 16252928 | bytes 2621440 | tf_op jit(solution)/shard_map/reduce_sum | solution.py:89
  444.6 129.8 %add_convert_fusion = bf16[128,128,32]{0,2,1:T(8,128)(2,1)} fusion(f32[128,128,32]{0,2,1:T(8,128)} %copy.192, bf16[128,128,32]{0,2,1:T(8,128)(2,1)S(1)} %copy-done.8, f32[128,1,32]{2,1,0:T(1,128)S(1)} %copy.183), kind=kOutput, calls=%fused_computation.25 | convolution fusion | flops 406847488 | bytes 4210688 | tf_op jit(solution)/shard_map/conv_general_dilated | solution.py:46
  580.5 5.0 all-to-all-start.1
  588.1 12.3 %all-to-all-done.1 = bf16[8,2048,32]{1,2,0:T(8,128)(2,1)S(1)} async-done(((bf16[8,2048,32]{1,2,0:T(8,128)(2,1)}), bf16[8,2048,32]{1,2,0:T(8,128)(2,1)S(1)}, u32[]{:S(2)}, u32[]{:S(2)}) %all-to-all-start.1) | async-done | bytes 1048608 | tf_op jit(solution)/shard_map/all_to_all | solution.py:129
  600.4 4.5 fusion.7
  (140 shorter events, 118.8 us)
Async XLA Ops:
  6.5 165.3 %all-gather.2.cloned.1.call-start = ((), (), s32[]{:S(2)}) async-start(), calls=%async_computation.2 | async-start | bytes 17825792 | tf_op jit(solution)/shard_map/all_gather | solution.py:105
  171.9 23.2 %copy-start.15 = (f32[3,3,256]{2,1,0:T(4,128)S(1)}, f32[3,3,256]{2,1,0:T(4,128)}, u32[]{:S(2)}) copy-start(f32[3,3,256]{2,1,0:T(4,128)} %param.12) | copy-start | bytes 27652
  190.1 1.6 copy-start.9
  191.9 7.9 %collective-permute-start = (bf16[2,3,256]{0,2,1:T(8,128)(2,1)S(1)}, bf16[2,3,256]{0,2,1:T(8,128)(2,1)S(1)}, u32[]{:S(2)}, u32[]{:S(2)}) collective-permute-start(bf16[2,3,256]{0,2,1:T(8,128)(2,1)S(1)} %bitcast.88), channel_id=1, source_target_pairs={{0,16},{16,32},{32,48},{48,64},{64,80},{80,96},{96,112},{1,17},{17... | collective-permute-start | bytes 9224 | tf_op jit(solution)/shard_map/ppermute | solution.py:15
  208.1 3.3 copy-start
  208.1 6.7 %copy-start.14 = (bf16[128,256]{1,0:T(8,128)(2,1)S(1)}, bf16[128,256]{1,0:T(8,128)(2,1)}, u32[]{:S(2)}) copy-start(bf16[128,256]{1,0:T(8,128)(2,1)} %param.13) | copy-start | bytes 196612
  211.4 9.9 %collective-permute-start.1 = (bf16[127,256]{0,1:T(8,128)(2,1)S(1)}, bf16[127,256]{0,1:T(8,128)(2,1)S(1)}, u32[]{:S(2)}, u32[]{:S(2)}) collective-permute-start(bf16[127,256]{0,1:T(8,128)(2,1)S(1)} %slice_bitcast_fusion.1), channel_id=1, source_target_pairs={{0,16},{16,32},{32,48},{48,64},{64,80},{80,96},{96,112},{1,17},{17... | collective-permute-start | bytes 195080 | tf_op jit(solution)/shard_map/ppermute | solution.py:15
  278.6 9.1 %copy-start.16 = (f32[16,256]{1,0:T(8,128)S(1)}, f32[16,256]{1,0:T(8,128)}, u32[]{:S(2)}) copy-start(f32[16,256]{1,0:T(8,128)} %param.15) | copy-start | bytes 49156
  278.6 9.1 %copy-start.17 = (f32[16,256]{1,0:T(8,128)S(1)}, f32[16,256]{1,0:T(8,128)}, u32[]{:S(2)}) copy-start(f32[16,256]{1,0:T(8,128)} %param.16) | copy-start | bytes 49156
  282.9 18.4 %all-to-all-start = ((bf16[2048,8,32]{0,2,1:T(8,128)(2,1)}), bf16[2048,8,32]{0,2,1:T(8,128)(2,1)S(1)}, u32[]{:S(2)}, u32[]{:S(2)}) async-start(bf16[2048,8,32]{0,2,1:T(8,128)(2,1)} %multiply_convert_fusion), calls=%async_computation | async-start | bytes 2097152 | tf_op jit(solution)/shard_map/all_to_all | solution.py:122
  321.6 23.6 %copy-start.1 = (f32[64,16,32]{0,2,1:T(8,128)}, f32[64,16,32]{0,2,1:T(8,128)S(1)}, u32[]{:S(2)}) copy-start(f32[64,16,32]{0,2,1:T(8,128)S(1)} %multiply_add_fusion.7) | copy-start | bytes 393220
  346.4 3.4 copy-start.5
  370.9 2.5 copy-start.12
  373.5 5.1 copy-start.6
  377.5 3.5 copy-start.4
  378.6 2.2 copy-start.13
  380.9 11.7 %copy-start.3 = (f32[32,16,32]{0,2,1:T(8,128)S(1)}, f32[32,16,32]{0,2,1:T(8,128)}, u32[]{:S(2)}) copy-start(f32[32,16,32]{0,2,1:T(8,128)} %multiply_add_fusion.6) | copy-start | bytes 196612
  391.5 5.3 copy-start.2
  395.7 23.6 %copy-start.10 = (f32[63,16,32]{2,1,0:T(8,128)S(1)}, f32[63,16,32]{2,1,0:T(8,128)}, u32[]{:S(2)}) copy-start(f32[63,16,32]{2,1,0:T(8,128)} %slice.248) | copy-start | bytes 387076
  397.0 24.5 %slice-start = ((f32[128,16,32]{2,1,0:T(8,128)}), f32[1,16,32]{2,1,0:T(8,128)S(1)}, s32[]{:S(2)}) async-start(f32[128,16,32]{2,1,0:T(8,128)} %copy-done.7), calls=%async_computation.3 | async-start | bytes 16384 | tf_op jit(solution)/shard_map/slice | solution.py:75
  420.3 6.8 %copy-start.11 = (f32[128,16,32]{0,2,1:T(8,128)S(1)}, f32[128,16,32]{0,2,1:T(8,128)}, u32[]{:S(2)}) copy-start(f32[128,16,32]{0,2,1:T(8,128)} %pad.126) | copy-start | bytes 786436
  441.1 3.5 copy-start.8
  580.5 19.9 %all-to-all-start.1 = ((bf16[8,2048,32]{1,2,0:T(8,128)(2,1)}), bf16[8,2048,32]{1,2,0:T(8,128)(2,1)S(1)}, u32[]{:S(2)}, u32[]{:S(2)}) async-start(bf16[8,2048,32]{1,2,0:T(8,128)(2,1)} %copy.194), calls=%async_computation.1 | async-start | bytes 2097152 | tf_op jit(solution)/shard_map/all_to_all | solution.py:129
  585.5 14.9 %copy-start.18 = (f32[256]{0:T(256)S(1)}, f32[256]{0:T(256)}, u32[]{:S(2)}) copy-start(f32[256]{0:T(256)} %param.17) | copy-start | bytes 3076
  (2 other events, 1.7 us)
Sparse Core Ops, SparseCore 0:
  46.2 125.6 all-gather.1
where the time goes:
time: 617 us; the launch traced here: 613 us
  matrix products  196 us (32%)
  local copies, waits for them, and re-layouts  142 us (23%)
  waiting for transfers between devices  140 us (23%)
  other arithmetic  69.7 us (11%)
  blocking collectives  34.7 us (6%)
  starting transfers between devices  16.4 us (3%)
  between operations  14 us (2%)
    conv_general_dilated x2, matrix products, depthwise(): lax.conv_general_dilated(signal, kernel, (1,), ((front, 0),), dimension_n...  178 us
    all_gather x1, waiting for transfers between devices, on_device(): lax.all_gather(normed, 'chan', axis=1, tiled=True)  117 us
    slice x21, local copies, waits for them, and re-layouts, modal_local(): lax.associative_scan(combine_states, (step_decay, block_ends), axis=0)  44.4 us
    unnamed x48, local copies, waits for them, and re-layouts  37.7 us
    psum x1, blocking collectives, on_device(): squares = lax.psum(jnp.sum(values * values, axis=1), 'chan')  34.7 us
    pad x10, local copies, waits for them, and re-layouts, modal_local(): lax.associative_scan(combine_states, (step_decay, block_ends), axis=0)  28.4 us
    dot_general x1, matrix products, on_device(): jnp.dot(lax.all_gather(normed, 'chan', axis=1, tiled=True), flat_weight,...  18.2 us
    add x12, other arithmetic, combine_states(): return (earlier[0] * later[0], later[0] * earlier[1] + later[1])  14.2 us
  transfers between devices with their start and end apart: 5, of which 3 were waited for; matrix products, arithmetic and copies ran while one was open for 4% of the time, Pallas kernels for 0%

commit v1 on v0

--- a/solution.py
+++ b/solution.py
@@ -96,7 +96,7 @@
     tokens, channels = resid.shape
     flat_weight = feat_weight.reshape(feat_weight.shape[0], 3 * channels)
     values = resid.astype(jnp.float32)
-    squares = lax.psum(jnp.sum(values * values, axis=1), "chan")
+    squares = jnp.sum(lax.all_gather(jnp.sum(values * values, axis=1), "chan"), axis=0)
     inv_scale = lax.rsqrt(squares / D + norm_epsilon)
     normed = (values * inv_scale[:, None] * norm_gain.astype(jnp.float32)[None]).astype(
         jnp.bfloat16

time: 617 us -> 602 us (0.976)
  blocking collectives: 34.7 us -> 26 us
    psum x1 -> x0, blocking collectives: 34.7 us -> none  [on_device(): squares = lax.psum(jnp.sum(values * values, axis=1), 'chan')]
    all_gather x0 -> x1, blocking collectives: none -> 26 us  [on_device(): lax.all_gather(jnp.sum(values * values, axis=1), 'chan')]
    unnamed x48 -> x50, local copies, waits for them, and re-layouts: 37.7 us -> 37.8 us
where the time goes in v1:
time: 602 us; the launch traced here: 598 us
  matrix products  196 us (33%)
  local copies, waits for them, and re-layouts  143 us (24%)
  waiting for transfers between devices  135 us (22%)
  other arithmetic  68.6 us (11%)
  blocking collectives  26 us (4%)
  starting transfers between devices  16.5 us (3%)
  between operations  14 us (2%)
    conv_general_dilated x2, matrix products, depthwise(): lax.conv_general_dilated(signal, kernel, (1,), ((front, 0),), dimension_n...  178 us
    all_gather x1, waiting for transfers between devices, on_device(): lax.all_gather(normed, 'chan', axis=1, tiled=True)  112 us
    slice x21, local copies, waits for them, and re-layouts, modal_local(): lax.associative_scan(combine_states, (step_decay, block_ends), axis=0)  44.5 us
    unnamed x50, local copies, waits for them, and re-layouts  37.8 us
    pad x10, local copies, waits for them, and re-layouts, modal_local(): lax.associative_scan(combine_states, (step_decay, block_ends), axis=0)  28.4 us
    all_gather x1, blocking collectives, on_device(): lax.all_gather(jnp.sum(values * values, axis=1), 'chan')  26 us
    dot_general x1, matrix products, on_device(): jnp.dot(lax.all_gather(normed, 'chan', axis=1, tiled=True), flat_weight,...  18.2 us
    add x12, other arithmetic, combine_states(): return (earlier[0] * later[0], later[0] * earlier[1] + later[1])  14.2 us
  transfers between devices with their start and end apart: 5, of which 3 were waited for; matrix products, arithmetic and copies ran while one was open for 4% of the time, Pallas kernels for 0%

profile of v1, /device:TPU:1, one launch (start us, length us, event | category | flops | bytes accessed | tf_op | source)
XLA Modules:
  0.0 598.5 jit_solution(10004136561236505842)
XLA Ops:
  8.2 26.0 %all-gather = f32[32768]{0:T(1024)S(1)} all-gather(f32[2048]{0:T(1024)S(1)} %fusion.2), channel_id=2, replica_groups=mesh['seq'=8,'chan'=16] {'chan'}, dimensions={0}, use_global_device_ids=true | all-gather | bytes 139264 | tf_op jit(solution)/shard_map/all_gather | solution.py:99
  36.3 8.8 %copy.172 = bf16[4096,3,256]{0,2,1:T(8,128)(2,1)} copy(bf16[4096,3,256]{2,0,1:T(8,128)(2,1)} %param.11) | data formatting | bytes 12582912 | tf_op args[2]
  45.1 111.9 %all-gather.3.cloned.1.call-done = bf16[2048,4096]{1,0:T(8,128)(2,1)} async-done(((bf16[2048,256]{1,0:T(8,128)(2,1)}), bf16[2048,4096]{1,0:T(8,128)(2,1)}) %all-gather.3.cloned.1.call-update) | async-done | bytes 16777232 | tf_op jit(solution)/shard_map/all_gather | solution.py:105
  157.0 18.2 %convolution_convert_fusion = bf16[2048,768]{1,0:T(8,128)(2,1)S(1)} fusion(bf16[2048,4096]{1,0:T(8,128)(2,1)} %all-gather.3.cloned.1.call-done, bf16[4096,768]{0,1:T(8,128)(2,1)} %bitcast.84), kind=kOutput, calls=%fused_computation.3 | convolution fusion | flops 12886474752 | bytes 26214400 | tf_op jit(solution)/shard_map/dot_general | solution.py:104
  180.3 4.8 copy.173
  185.0 8.1 %multiply_add_fusion = f32[2048,3,256]{0,2,1:T(8,128)S(1)} fusion(bf16[2048,3,256]{0,2,1:T(8,128)(2,1)} %bitcast.76, bf16[2,3,256]{0,2,1:T(8,128)(2,1)S(1)} %collective-permute-done, f32[3,256]{1,0:T(4,128)S(1)} %get-tuple-element.19, f32[3,256]{1,0:T(4,128)S(1)} %get-tuple-element.20, f32[3,256]{1,0:T(4,128)S(1)} %get-tuple-element.18), kind=kLoop, calls=%fused_computation.2 | loop fusion | flops 22020096 | bytes 9449472 | tf_op jit(solution)/shard_map/add | solution.py:36
  200.2 4.7 copy.171
  210.9 47.9 %fusion.17 = f32[8,272,256]{2,0,1:T(8,128)S(1)} fusion(pred[8,272]{0,1:T(8,128)(4,1)S(1)} %copy-done.20, bf16[128,1,256]{2,0,1:T(8,128)(2,1)S(1)} %bitcast.90, bf16[8,399,256]{2,0,1:T(8,128)(2,1)S(1)} %fusion.44), kind=kOutput, calls=%fused_computation.34 | convolution fusion | flops 143163392 | bytes 3930240 | tf_op jit(solution)/shard_map/conv_general_dilated | solution.py:46
  263.9 4.3 multiply_convert_fusion
  268.2 4.8 all-to-all-start
  276.0 10.7 %all-to-all-done = bf16[2048,8,32]{0,2,1:T(8,128)(2,1)S(1)} async-done(((bf16[2048,8,32]{0,2,1:T(8,128)(2,1)}), bf16[2048,8,32]{0,2,1:T(8,128)(2,1)S(1)}, u32[]{:S(2)}, u32[]{:S(2)}) %all-to-all-start) | async-done | bytes 1048608 | tf_op jit(solution)/shard_map/all_to_all | solution.py:122
  290.4 9.3 %multiply_reduce_fusion.1 = f32[128,16,32]{2,1,0:T(8,128)S(1)} fusion(f32[128,128,32]{1,2,0:T(8,128)S(1)} %copy.184, f32[128,16,32]{0,2,1:T(8,128)S(1)} %get-tuple-element.21), kind=kLoop, calls=%fused_computation.1 | loop fusion | flops 16711680 | bytes 2621440 | tf_op jit(solution)/shard_map/reduce_sum | solution.py:73
  307.0 3.7 slice.212
  310.7 3.8 slice.213
  348.2 4.5 slice.246
  368.1 6.6 %pad.51 = f32[16,16,32]{0,2,1:T(8,128)S(1)} pad(f32[8,16,32]{0,2,1:T(8,128)} %add.147, f32[]{:T(128)} %constant.12.clone.1), padding=1_0_1x0_0_0x0_0_0 | pad | bytes 49156 | tf_op jit(solution)/shard_map/pad | solution.py:75
  385.9 7.6 %pad.55 = f32[64,16,32]{0,2,1:T(8,128)S(1)} pad(f32[32,16,32]{0,2,1:T(8,128)} %add.151, f32[]{:T(128)} %constant.12.clone.1), padding=1_0_1x0_0_0x0_0_0 | pad | bytes 196612 | tf_op jit(solution)/shard_map/pad | solution.py:75
  394.2 10.6 %pad.126 = f32[128,16,32]{0,2,1:T(8,128)} pad(f32[64,16,32]{0,2,1:T(8,128)} %add.153, f32[]{:T(128)} %constant.12.clone.1), padding=1_0_1x0_0_0x0_0_0 | pad | bytes 393220
  407.2 5.3 pad.82
  413.3 13.2 %multiply_reduce_fusion = f32[128,128,32]{1,2,0:T(8,128)} fusion(f32[128,16,32]{2,1,0:T(8,128)S(1)} %copy.191, f32[128,16,32]{0,2,1:T(8,128)} %get-tuple-element.16), kind=kLoop, calls=%fused_computation | loop fusion | flops 16252928 | bytes 2621440 | tf_op jit(solution)/shard_map/reduce_sum | solution.py:89
  430.0 129.8 %add_convert_fusion = bf16[128,128,32]{0,2,1:T(8,128)(2,1)} fusion(f32[128,128,32]{0,2,1:T(8,128)} %copy.192, bf16[128,128,32]{0,2,1:T(8,128)(2,1)S(1)} %copy-done.9, f32[128,1,32]{2,1,0:T(1,128)S(1)} %copy.183), kind=kOutput, calls=%fused_computation.25 | convolution fusion | flops 406847488 | bytes 4210688 | tf_op jit(solution)/shard_map/conv_general_dilated | solution.py:46
  565.9 4.9 all-to-all-start.1
  573.4 12.3 %all-to-all-done.1 = bf16[8,2048,32]{1,2,0:T(8,128)(2,1)S(1)} async-done(((bf16[8,2048,32]{1,2,0:T(8,128)(2,1)}), bf16[8,2048,32]{1,2,0:T(8,128)(2,1)S(1)}, u32[]{:S(2)}, u32[]{:S(2)}) %all-to-all-start.1) | async-done | bytes 1048608 | tf_op jit(solution)/shard_map/all_to_all | solution.py:129
  585.8 4.5 fusion.7
  (144 shorter events, 118.0 us)
Async XLA Ops:
  6.5 28.4 %copy-start.8 = (bf16[2048,256]{1,0:T(8,128)(2,1)S(1)}, bf16[2048,256]{1,0:T(8,128)(2,1)}, u32[]{:S(2)}) copy-start(bf16[2048,256]{1,0:T(8,128)(2,1)} %param.9) | copy-start | bytes 3145732
  6.5 150.5 %all-gather.3.cloned.1.call-start = ((), (), s32[]{:S(2)}) async-start(), calls=%async_computation.2 | async-start | bytes 17825792 | tf_op jit(solution)/shard_map/all_gather | solution.py:105
  157.0 23.2 %copy-start.16 = (f32[3,3,256]{2,1,0:T(4,128)S(1)}, f32[3,3,256]{2,1,0:T(4,128)}, u32[]{:S(2)}) copy-start(f32[3,3,256]{2,1,0:T(4,128)} %param.12) | copy-start | bytes 27652
  177.0 8.0 %collective-permute-start = (bf16[2,3,256]{0,2,1:T(8,128)(2,1)S(1)}, bf16[2,3,256]{0,2,1:T(8,128)(2,1)S(1)}, u32[]{:S(2)}, u32[]{:S(2)}) collective-permute-start(bf16[2,3,256]{0,2,1:T(8,128)(2,1)S(1)} %bitcast.88), channel_id=1, source_target_pairs={{0,16},{16,32},{32,48},{48,64},{64,80},{80,96},{96,112},{1,17},{17... | collective-permute-start | bytes 9224 | tf_op jit(solution)/shard_map/ppermute | solution.py:15
  193.2 3.3 copy-start
  193.2 6.9 %copy-start.15 = (bf16[128,256]{1,0:T(8,128)(2,1)S(1)}, bf16[128,256]{1,0:T(8,128)(2,1)}, u32[]{:S(2)}) copy-start(bf16[128,256]{1,0:T(8,128)(2,1)} %param.13) | copy-start | bytes 196612
  196.5 10.1 %collective-permute-start.1 = (bf16[127,256]{0,1:T(8,128)(2,1)S(1)}, bf16[127,256]{0,1:T(8,128)(2,1)S(1)}, u32[]{:S(2)}, u32[]{:S(2)}) collective-permute-start(bf16[127,256]{0,1:T(8,128)(2,1)S(1)} %slice_bitcast_fusion.1), channel_id=1, source_target_pairs={{0,16},{16,32},{32,48},{48,64},{64,80},{80,96},{96,112},{1,17},{17... | collective-permute-start | bytes 195080 | tf_op jit(solution)/shard_map/ppermute | solution.py:15
  263.9 9.1 %copy-start.17 = (f32[16,256]{1,0:T(8,128)S(1)}, f32[16,256]{1,0:T(8,128)}, u32[]{:S(2)}) copy-start(f32[16,256]{1,0:T(8,128)} %param.15) | copy-start | bytes 49156
  263.9 9.1 %copy-start.18 = (f32[16,256]{1,0:T(8,128)S(1)}, f32[16,256]{1,0:T(8,128)}, u32[]{:S(2)}) copy-start(f32[16,256]{1,0:T(8,128)} %param.16) | copy-start | bytes 49156
  268.2 18.5 %all-to-all-start = ((bf16[2048,8,32]{0,2,1:T(8,128)(2,1)}), bf16[2048,8,32]{0,2,1:T(8,128)(2,1)S(1)}, u32[]{:S(2)}, u32[]{:S(2)}) async-start(bf16[2048,8,32]{0,2,1:T(8,128)(2,1)} %multiply_convert_fusion), calls=%async_computation | async-start | bytes 2097152 | tf_op jit(solution)/shard_map/all_to_all | solution.py:122
  307.0 23.7 %copy-start.1 = (f32[64,16,32]{0,2,1:T(8,128)}, f32[64,16,32]{0,2,1:T(8,128)S(1)}, u32[]{:S(2)}) copy-start(f32[64,16,32]{0,2,1:T(8,128)S(1)} %multiply_add_fusion.7) | copy-start | bytes 393220
  331.8 3.4 copy-start.5
  356.3 2.5 copy-start.13
  359.0 5.1 copy-start.6
  362.9 3.5 copy-start.4
  364.0 2.2 copy-start.14
  366.4 11.7 %copy-start.3 = (f32[32,16,32]{0,2,1:T(8,128)S(1)}, f32[32,16,32]{0,2,1:T(8,128)}, u32[]{:S(2)}) copy-start(f32[32,16,32]{0,2,1:T(8,128)} %multiply_add_fusion.6) | copy-start | bytes 196612
  377.0 5.3 copy-start.2
  381.1 23.6 %copy-start.11 = (f32[63,16,32]{2,1,0:T(8,128)S(1)}, f32[63,16,32]{2,1,0:T(8,128)}, u32[]{:S(2)}) copy-start(f32[63,16,32]{2,1,0:T(8,128)} %slice.248) | copy-start | bytes 387076
  382.4 24.4 %slice-start = ((f32[128,16,32]{2,1,0:T(8,128)}), f32[1,16,32]{2,1,0:T(8,128)S(1)}, s32[]{:S(2)}) async-start(f32[128,16,32]{2,1,0:T(8,128)} %copy-done.7), calls=%async_computation.3 | async-start | bytes 16384 | tf_op jit(solution)/shard_map/slice | solution.py:75
  405.8 6.8 %copy-start.12 = (f32[128,16,32]{0,2,1:T(8,128)S(1)}, f32[128,16,32]{0,2,1:T(8,128)}, u32[]{:S(2)}) copy-start(f32[128,16,32]{0,2,1:T(8,128)} %pad.126) | copy-start | bytes 786436
  426.5 3.5 copy-start.9
  565.9 19.9 %all-to-all-start.1 = ((bf16[8,2048,32]{1,2,0:T(8,128)(2,1)}), bf16[8,2048,32]{1,2,0:T(8,128)(2,1)S(1)}, u32[]{:S(2)}, u32[]{:S(2)}) async-start(bf16[8,2048,32]{1,2,0:T(8,128)(2,1)} %copy.194), calls=%async_computation.1 | async-start | bytes 2097152 | tf_op jit(solution)/shard_map/all_to_all | solution.py:129
  570.8 14.9 %copy-start.19 = (f32[256]{0:T(256)S(1)}, f32[256]{0:T(256)}, u32[]{:S(2)}) copy-start(f32[256]{0:T(256)} %param.17) | copy-start | bytes 3076
  (3 other events, 3.4 us)
Sparse Core Ops, SparseCore 0:
  36.4 120.5 all-gather.2
